TPU v7x, 512 devices: a whole 4x4x16 slice. The times are simulated.
512 devices in a mesh: dp: 8 (over y_hi, x), feat: 64 (over y_lo, z, core).
Axes of the slice: x: 4, y: 4 (y_hi: 2, y_lo: 2; y = y_hi * 2 + y_lo), z: 16, core: 2. Of those that a mesh axis runs over, the one named last changes fastest.
Arguments:
- residuals: bfloat16 [384, 2, 8192], P('feat', None, 'dp'), may hold values from -6 to 6
- enc_w: bfloat16 [2, 8192, 16384], P(None, 'dp', 'feat'), may hold values from -0.046875 to 0.046875
- enc_b: float32 [16384], P('feat'), may hold values from 0.5 to 3
- dec_w: bfloat16 [2, 16384, 8192], P(None, 'feat', 'dp'), may hold values from -0.75 to 0.75
- dec_b: float32 [2, 8192], P(None, 'dp'), may hold values from -3 to 3
- active: int32 [384, 64], replicated, may hold values from 0 to 16383, all different within a row
Outputs:
- recon: bfloat16 [384, 2, 8192], P('feat', None, 'dp')
- enc_grad: bfloat16 [2, 8192, 16384], P(None, 'dp', 'feat')
- enc_bias_grad: float32 [16384], P('feat')
- dec_grad: bfloat16 [2, 16384, 8192], P(None, 'feat', 'dp')
- dec_bias_grad: float32 [2, 8192], P(None, 'dp')
Inputs may be any that keep to these rules, and one draw needn't show every extreme that they name: Each row of active names 64 different features, and every feature is named by some row.
All inputs are finite; a program needn't handle non-finite values.
Results may differ from a plain program's by a relative error of at most 0.0062.
Values may be sent and summed in bfloat16 or wider, within the bound.
A program may use at most 64 MiB of HBM per device.

v0:
```python
import math

import jax
import jax.numpy as jnp
from jax import lax
from jax.sharding import PartitionSpec as P


def feature_mask(active, first_feature, feat_dev):
    columns = first_feature + lax.iota(jnp.int32, feat_dev)
    total_rows, top_count = active.shape
    block_rows = math.gcd(total_rows, 64)
    grouped = active.reshape(total_rows // block_rows, block_rows, top_count)

    def one_block(row_group):
        return jnp.any(row_group[:, :, None] == columns[None, None, :], axis=1).astype(jnp.float32)

    return lax.map(one_block, grouped).reshape(total_rows, feat_dev)


def on_device(residuals, enc_w, enc_b, dec_w, dec_b, active):
    n_layers, width_dev, feat_dev = enc_w.shape
    gathered = lax.all_gather(residuals, "feat", axis=0, tiled=True)
    total_rows = gathered.shape[0]
    flat_in = gathered.reshape(total_rows, n_layers * width_dev)
    partial_value = jnp.dot(
        flat_in, enc_w.reshape(n_layers * width_dev, feat_dev), preferred_element_type=jnp.float32
    )
    pre_act = lax.psum(partial_value, "dp") + enc_b
    first_feature = lax.axis_index("feat") * feat_dev
    mask_table = feature_mask(active, first_feature, feat_dev)
    activation = (jnp.maximum(pre_act, 0.0) * mask_table).astype(jnp.bfloat16)
    rows_act = activation
    summed = lax.psum_scatter(
        jnp.einsum("tf,lfd->tld", rows_act, dec_w, preferred_element_type=jnp.float32),
        "feat",
        scatter_dimension=0,
        tiled=True,
    )
    recon_full = summed + dec_b[None]
    recon = recon_full.astype(jnp.bfloat16)
    resid_grad = ((recon_full - residuals.astype(jnp.float32)) * 0.25).astype(jnp.bfloat16)
    dec_bias_grad = lax.psum(jnp.sum(resid_grad.astype(jnp.float32), axis=0), "feat")
    shard_rows = lax.all_gather(resid_grad, "feat", axis=0, tiled=True)
    rows_act = activation
    dec_part = jnp.einsum("tf,tld->lfd", rows_act, shard_rows, preferred_element_type=jnp.float32)
    rows_grad = jnp.einsum("tld,lfd->tf", shard_rows, dec_w, preferred_element_type=jnp.float32)
    act_grad = lax.psum(rows_grad, "dp")
    pre_grad = jnp.where(activation > 0, act_grad, 0.0).astype(jnp.bfloat16)
    enc_bias_grad = jnp.sum(pre_grad.astype(jnp.float32), axis=0)
    enc_full = lax.dot_general(
        flat_in, pre_grad, (((0,), (0,)), ((), ())), preferred_element_type=jnp.float32
    )
    enc_grad = enc_full.reshape(n_layers, width_dev, feat_dev).astype(jnp.bfloat16)
    return (recon, enc_grad, enc_bias_grad, dec_part.astype(jnp.bfloat16), dec_bias_grad)


def solution(mesh):
    return jax.shard_map(
        on_device,
        mesh=mesh,
        in_specs=(
            P("feat", None, "dp"),
            P(None, "dp", "feat"),
            P("feat"),
            P(None, "feat", "dp"),
            P(None, "dp"),
            P(),
        ),
        out_specs=(
            P("feat", None, "dp"),
            P(None, "dp", "feat"),
            P("feat"),
            P(None, "feat", "dp"),
            P(None, "dp"),
        ),
        check_vma=False,
    )
```

profile of v0, /device:TPU:1, one launch (start us, length us, event | category | flops | bytes accessed | tf_op | source)
XLA Modules:
  0.0 862.5 jit_solution(2838763191016575245)
XLA Ops:
  7.2 0.0 all-gather.3.cloned.1.call-start
  7.2 0.7 all-gather.3.cloned.1.call-update
  7.9 0.0 all-reduce.5.cloned.1.call-start
  8.0 1.0 copy.33
  9.0 128.5 %all-gather.3.cloned.1.call-done = bf16[384,2,1024]{2,1,0:T(2,128)(2,1)} async-done(((bf16[6,2,1024]{2,1,0:T(2,128)(2,1)}), bf16[384,2,1024]{2,1,0:T(2,128)(2,1)}) %all-gather.3.cloned.1.call-update) | async-done | bytes 1572880 | tf_op jit(solution)/shard_map/all_gather | solution.py:23
  137.5 3.7 copy.36
  141.3 2.6 convolution_bitcast_fusion
  143.9 0.0 all-reduce.7.cloned.1.call-start
  143.9 4.8 while.11
  144.0 0.7 compare_reduce_fusion.2
  144.8 0.7 compare_reduce_fusion.2
  145.6 0.7 compare_reduce_fusion.2
  146.4 0.7 compare_reduce_fusion.2
  147.2 0.7 compare_reduce_fusion.2
  148.0 0.7 compare_reduce_fusion.2
  148.7 86.6 %all-reduce.5.cloned.1.call-done = f32[384,256]{1,0:T(8,128)} async-done(((f32[384,256]{1,0:T(8,128)}), f32[384,256]{1,0:T(8,128)}) %all-reduce.5.cloned.1.call-update) | async-done | bytes 393232 | tf_op jit(solution)/shard_map/psum | solution.py:29
  235.3 1.1 fusion.12
  236.4 0.6 fusion.14
  236.9 4.1 copy.34
  241.1 0.0 all-gather.5.cloned.1.call-start
  241.1 1.3 dynamic-slice
  243.1 446.3 %all-reduce.7.cloned.1.call-done = f32[384,2,1024]{2,1,0:T(2,128)} async-done(((f32[384,2,1024]{2,1,0:T(2,128)}), f32[384,2,1024]{2,1,0:T(2,128)}) %all-reduce.7.cloned.1.call-update) | async-done | bytes 3145744
  689.3 1.5 convert_reduce_fusion.1
  690.8 107.4 %psum.23 = f32[2,1024]{1,0:T(2,128)} all-reduce(f32[2,1024]{1,0:T(2,128)S(1)} %get-tuple-element.67), channel_id=1, replica_groups=mesh['dp'=8,'feat'=64] {'feat'}, use_global_device_ids=true, to_apply=%region_8.9 | all-reduce | flops 2048 | bytes 16384 | tf_op jit(solution)/shard_map/psum | solution.py:43
  798.3 9.2 %all-gather.5.cloned.1.call-done = bf16[384,2,1024]{2,1,0:T(2,128)(2,1)} async-done(((bf16[6,2,1024]{2,1,0:T(2,128)(2,1)}), bf16[384,2,1024]{2,1,0:T(2,128)(2,1)}) %all-gather.5.cloned.1.call-update) | async-done | bytes 1572880 | tf_op jit(solution)/shard_map/all_gather | solution.py:44
  807.5 2.0 fusion.9
  809.5 38.3 %all-reduce.8 = bf16[384,256]{1,0:T(8,128)(2,1)S(1)} all-reduce(f32[384,256]{1,0:T(8,128)S(1)} %fusion.9), channel_id=1, replica_groups=mesh['dp'=8,'feat'=64] {'dp'}, use_global_device_ids=true, to_apply=%region_5.6 | all-reduce | flops 98304 | bytes 589824 | tf_op jit(solution)/shard_map/psum | solution.py:48
  847.8 0.7 convert_reduce_fusion
  848.5 1.7 fusion.2
  850.2 2.3 copy.40
  852.5 2.2 fusion.6
  854.7 1.3 copy.39
  (30 shorter events, 0.2 us)
Async XLA Ops:
  7.2 229.2 %copy-start = (bf16[2,256,1024]{2,1,0:T(8,128)(2,1)S(1)}, bf16[2,256,1024]{2,1,0:T(8,128)(2,1)}, u32[]{:S(2)}) copy-start(bf16[2,256,1024]{2,1,0:T(8,128)(2,1)} %param.11) | copy-start | bytes 3145732
  7.2 130.3 %all-gather.3.cloned.1.call-start = ((), (), s32[]{:S(2)}) async-start(), calls=%async_computation | async-start | bytes 1597440 | tf_op jit(solution)/shard_map/all_gather | solution.py:23
  7.9 227.4 %all-reduce.5.cloned.1.call-start = ((), (), s32[]{:S(2)}) async-start(), calls=%async_computation.1 | async-start | bytes 786432 | tf_op jit(solution)/shard_map/psum | solution.py:29
  141.3 94.0 %copy-start.3 = (f32[256]{0:T(256)S(1)}, f32[256]{0:T(256)}, u32[]{:S(2)}) copy-start(f32[256]{0:T(256)} %param.10) | copy-start | bytes 3076
  143.9 545.4 %all-reduce.7.cloned.1.call-start = ((), (), s32[]{:S(2)}) async-start(), calls=%async_computation.3 | async-start | bytes 6291456
  241.1 448.3 %copy-start.1 = (bf16[6,2,1024]{2,1,0:T(2,128)(2,1)S(1)}, bf16[6,2,1024]{2,1,0:T(2,128)(2,1)}, u32[]{:S(2)}) copy-start(bf16[6,2,1024]{2,1,0:T(2,128)(2,1)} %param.8) | copy-start | bytes 73732
  241.1 448.3 %copy-start.2 = (f32[2,1024]{1,0:T(2,128)S(1)}, f32[2,1024]{1,0:T(2,128)}, u32[]{:S(2)}) copy-start(f32[2,1024]{1,0:T(2,128)} %param.12) | copy-start | bytes 24580
  241.1 566.4 %all-gather.5.cloned.1.call-start = ((), (), s32[]{:S(2)}) async-start(), calls=%async_computation.2 | async-start | bytes 1597440 | tf_op jit(solution)/shard_map/all_gather | solution.py:44
Sparse Core Ops, SparseCore 0:
  10.1 127.3 all-gather.2
  144.0 91.2 all-reduce.4
  241.2 448.0 all-reduce.6
  691.9 115.4 all-gather.4
where the time goes:
time: 869 us; the launch traced here: 863 us
  waiting for transfers between devices  671 us (77%)
  blocking collectives  146 us (17%)
  between operations  14.5 us (2%)
  local copies, waits for them, and re-layouts  13.8 us (2%)
  matrix products  9.1 us (1%)
    unnamed x5, waiting for transfers between devices  447 us
    all_gather x1, waiting for transfers between devices, on_device(): gathered = lax.all_gather(residuals, 'feat', axis=0, tiled=True)  129 us
    psum x1, blocking collectives, on_device(): lax.psum(jnp.sum(resid_grad.astype(jnp.float32), axis=0), 'feat')  107 us
    psum x1, waiting for transfers between devices, on_device(): pre_act = lax.psum(partial_value, 'dp') + enc_b  86.6 us
    psum x1, blocking collectives, on_device(): act_grad = lax.psum(rows_grad, 'dp')  38.3 us
  transfers between devices with their start and end apart: 4, of which 4 were waited for; matrix products, arithmetic and copies ran while one was open for 1% of the time, Pallas kernels for 0%

commit v1 on v0

v1 whole, which is shorter than its diff:
```python
import functools

import jax
import jax.numpy as jnp
from jax import lax
from jax.experimental import pallas as pl
from jax.experimental.pallas import tpu as pltpu
from jax.sharding import PartitionSpec as P

MESH = pl.DeviceIdType.MESH
NZ = 16
F32 = jnp.float32
BF16 = jnp.bfloat16


def rdma(src, dst, send, recv, **where):
    return pltpu.make_async_remote_copy(
        src_ref=src, dst_ref=dst, send_sem=send, recv_sem=recv, device_id=where, device_id_type=MESH
    )


def place():
    me = lax.axis_index("feat")
    return me // 32, (me // 2) % NZ, me % 2


def feat_of(y, z, c):
    return (y * NZ + z) * 2 + c


def turn(i):
    odd = i % 2
    return (odd * ((i + 1) // 2) + (1 - odd) * (NZ - i // 2)) % NZ


def greet_feat():
    y, z, c = place()
    barrier = pltpu.get_barrier_semaphore()

    def signal(target):
        pl.semaphore_signal(barrier, inc=1, device_id={"feat": target}, device_id_type=MESH)

    def one(i, carry):
        signal(feat_of(y, (z + i) % NZ, c))
        return carry

    lax.fori_loop(1, NZ, one, 0)
    signal(feat_of(1 - y, z, c))
    signal(feat_of(y, z, 1 - c))
    signal(feat_of(1 - y, z, 1 - c))
    pl.semaphore_wait(barrier, NZ + 2)


def gather_feat(out, sems):
    zs, zr, ys, yr, cs, cr, ds, dr = sems
    y, z, c = place()
    half = out.shape[3] // 2

    def chunk(layer, zz, part):
        return out.at[layer, zz, :, pl.ds(pl.multiple_of(part * half, half), half)]

    def z_copy(s):
        return rdma(chunk(y, z, c), chunk(y, z, c), zs.at[s], zr.at[s], feat=feat_of(y, (z + s) % NZ, c))

    def z_arrival(s):
        piece = chunk(y, (z + NZ - s) % NZ, c)
        return rdma(piece, piece, zs.at[s], zr.at[s], feat=feat_of(y, (z + s) % NZ, c))

    def y_copy(s, layer):
        piece = chunk(layer, (z + NZ - s) % NZ, c)
        return rdma(piece, piece, ys.at[s], yr.at[s], feat=feat_of(1 - y, z, c))

    def c_copy(s, part):
        piece = chunk(y, (z + NZ - s) % NZ, part)
        return rdma(piece, piece, cs.at[s], cr.at[s], feat=feat_of(y, z, 1 - c))

    def d_copy(s, part):
        piece = chunk(1 - y, (z + NZ - s) % NZ, part)
        return rdma(piece, piece, ds.at[s], dr.at[s], feat=feat_of(y, z, 1 - c))

    def send(i, carry):
        z_copy(turn(NZ - i)).start()
        return carry

    def forward(i, carry):
        s = turn(i)

        @pl.when(i > 0)
        def _():
            z_arrival(s).wait_recv()

        y_copy(s, y).start()
        c_copy(s, c).start()

        @pl.when(i > 0)
        def _():
            before = turn(i - 1)
            y_copy(before, 1 - y).wait_recv()
            d_copy(before, c).start()

        return carry

    def finish(s, carry):
        @pl.when(s > 0)
        def _():
            z_copy(s).wait_send()

        y_copy(s, y).wait_send()
        c_copy(s, c).wait_send()
        d_copy(s, c).wait_send()
        c_copy(s, 1 - c).wait_recv()
        d_copy(s, 1 - c).wait_recv()
        return carry

    lax.fori_loop(1, NZ, send, 0)
    lax.fori_loop(0, NZ, forward, 0)
    last = turn(NZ - 1)
    y_copy(last, 1 - y).wait_recv()
    d_copy(last, c).start()
    lax.fori_loop(0, NZ, finish, 0)


GATHER_SEMS = [pltpu.SemaphoreType.DMA((NZ,))] * 8


def others(y, z, c):
    return (feat_of(1 - y, z, c), 1 - y, c), (feat_of(y, z, 1 - c), y, 1 - c), (feat_of(1 - y, z, 1 - c), 1 - y, 1 - c)


def gather_kernel(x_ref, out, got, gs, gr, *sems):
    y, z, c = place()
    half = x_ref.shape[2] // 2

    def cols(part):
        return pl.ds(pl.multiple_of(part * half, half), half)

    greet_feat()
    copies = [
        rdma(x_ref.at[yy, :, cols(cc)], got.at[k], gs.at[k], gr.at[k], feat=peer)
        for k, (peer, yy, cc) in enumerate(others(y, z, c))
    ]
    for copy in copies:
        copy.start()
    total = x_ref[y, :, cols(c)].astype(F32)
    for k, copy in enumerate(copies):
        copy.wait_recv()
        total = total + got[k].astype(F32)
    out[y, z, :, cols(c)] = total.astype(BF16)
    gather_feat(out, sems)
    for copy in copies:
        copy.wait_send()


def reduce_kernel(part, resid, bias, grad, recon, ra, rb, ry, rz, sy, sz, ss, sr, ws, wr, vs, vr, gs, gr, *sems):
    y, z, c = place()
    half = part.shape[3] // 2

    def cols(p):
        return pl.ds(pl.multiple_of(p * half, half), half)

    greet_feat()
    sibling = feat_of(y, z, 1 - c)
    first = rdma(part.at[1 - y, :, :, cols(1 - c)], ra, ss.at[0], sr.at[0], feat=sibling)
    second = rdma(part.at[y, :, :, cols(1 - c)], rb, ss.at[1], sr.at[1], feat=sibling)
    first.start()
    second.start()

    def y_copy(zz):
        return rdma(sy.at[zz], ry.at[zz], ws.at[zz], wr.at[zz], feat=feat_of(1 - y, z, c))

    def z_copy(s):
        return rdma(sz.at[s], rz.at[s], vs.at[s], vr.at[s], feat=feat_of(y, (z + s) % NZ, c))

    def to_y(i, carry):
        zz = (z + turn(NZ - 1 - i)) % NZ
        sy[zz] = (part[1 - y, zz, :, cols(c)] + ra[zz]).astype(BF16)
        y_copy(zz).start()
        return carry

    def to_z(i, carry):
        s = turn(NZ - 1 - i)
        zz = (z + s) % NZ
        y_copy(zz).wait_recv()
        sz[s] = (part[y, zz, :, cols(c)] + rb[zz] + ry[zz].astype(F32)).astype(BF16)
        z_copy(s).start()
        return carry

    first.wait_recv()
    lax.fori_loop(0, NZ, to_y, 0)
    second.wait_recv()
    lax.fori_loop(0, NZ - 1, to_z, 0)
    y_copy(z).wait_recv()
    total = part[y, z, :, cols(c)] + rb[z] + ry[z].astype(F32)

    def add(i, total):
        s = turn(i)
        z_copy(s).wait_recv()
        return total + rz[s].astype(F32)

    total = lax.fori_loop(1, NZ, add, total)
    full = total + bias[y, :, cols(c)]
    grad[y, z, :, cols(c)] = ((full - resid[y, z, :, cols(c)].astype(F32)) * 0.25).astype(BF16)
    recon[y, :, cols(c)] = full.astype(BF16)
    gather_feat(grad, sems)
    mine = recon.at[y, :, cols(c)]
    copies = [rdma(mine, mine, gs.at[k], gr.at[k], feat=peer) for k, (peer, _, _) in enumerate(others(y, z, c))]
    for copy in copies:
        copy.start()
    first.wait_send()
    second.wait_send()

    def drain(i, carry):
        y_copy(i).wait_send()

        @pl.when(i > 0)
        def _():
            z_copy(i).wait_send()

        return carry

    lax.fori_loop(0, NZ, drain, 0)
    for k, (peer, yy, cc) in enumerate(others(y, z, c)):
        copies[k].wait_send()
        piece = recon.at[yy, :, cols(cc)]
        rdma(piece, piece, gs.at[k], gr.at[k], feat=peer).wait_recv()


def dp_sum_kernel(finish, n, part, *refs):
    extra, (out, got, ps, pr, qs, qr) = refs[:-6], refs[-6:]
    me = lax.axis_index("dp")
    barrier = pltpu.get_barrier_semaphore()
    for s in range(1, n):
        pl.semaphore_signal(barrier, inc=1, device_id={"dp": (me + s) % n}, device_id_type=MESH)
    pl.semaphore_wait(barrier, n - 1)
    copies = [
        rdma(part.at[(me + s) % n], got.at[s], ps.at[s], pr.at[s], dp=(me + s) % n) for s in range(1, n)
    ]
    for copy in copies:
        copy.start()
    total = part[me]
    for s, copy in enumerate(copies, 1):
        copy.wait_recv()
        total = total + got[s]
    out[me] = finish(total, *[ref[...] for ref in extra])
    backs = [rdma(out.at[me], out.at[me], qs.at[s], qr.at[s], dp=(me + s) % n) for s in range(1, n)]
    for back in backs:
        back.start()
    for s in range(1, n):
        copies[s - 1].wait_send()
        backs[s - 1].wait_send()
        piece = out.at[(me + n - s) % n]
        rdma(piece, piece, qs.at[s], qr.at[s], dp=(me + s) % n).wait_recv()


def vmem(count):
    return [pl.BlockSpec(memory_space=pltpu.VMEM)] * count


def params(number):
    return pltpu.CompilerParams(collective_id=number, has_side_effects=True, vmem_limit_bytes=48 * 1024 * 1024)


def dp_sum(number, finish, part, *extra):
    n, rows, feats = part.shape
    return pl.pallas_call(
        functools.partial(dp_sum_kernel, finish, n),
        out_shape=jax.ShapeDtypeStruct(part.shape, BF16),
        in_specs=vmem(1 + len(extra)),
        out_specs=vmem(1)[0],
        scratch_shapes=[pltpu.VMEM(part.shape, F32)] + [pltpu.SemaphoreType.DMA((n,))] * 4,
        compiler_params=params(number),
    )(part, *extra)


def activate(total, bias, mask):
    return (jnp.maximum(total + bias, 0.0) * mask).astype(BF16)


def pass_grad(total, activation):
    return jnp.where(activation.astype(F32) > 0, total, 0.0).astype(BF16)


def on_device(residuals, enc_w, enc_b, dec_w, dec_b, active):
    layers, width, feats = enc_w.shape
    own = residuals.shape[0]
    rows = 4 * own
    half = width // 2
    tokens = active.shape[0]
    feat = lax.axis_index("feat")
    dp = lax.axis_index("dp")
    quarter = (feat // 32) * 2 + feat % 2
    spread = lax.dynamic_update_slice(
        jnp.zeros((layers, rows, width), BF16), residuals.transpose(1, 0, 2), (0, quarter * own, 0)
    )
    sems3 = [pltpu.SemaphoreType.DMA((3,))] * 2
    gathered = pl.pallas_call(
        gather_kernel,
        out_shape=jax.ShapeDtypeStruct((layers, NZ, rows, width), BF16),
        in_specs=vmem(1),
        out_specs=vmem(1)[0],
        scratch_shapes=[pltpu.VMEM((3, rows, half), BF16)] + sems3 + GATHER_SEMS,
        compiler_params=params(0),
    )(spread)
    flat = gathered.reshape(layers, tokens, width)
    partial_value = jnp.dot(flat[0], enc_w[0], preferred_element_type=F32) + jnp.dot(
        flat[1], enc_w[1], preferred_element_type=F32
    )
    n = tokens // 48
    table = active.reshape(2, NZ, 2, own, -1).transpose(1, 0, 2, 3, 4).reshape(tokens, -1)
    table = lax.dynamic_slice_in_dim(table, dp * 48, 48, 0)
    columns = feat * feats + lax.iota(jnp.int32, feats)
    mask = jnp.any(table[:, :, None] == columns[None, None, :], axis=1).astype(F32)
    activation = dp_sum(1, activate, partial_value.reshape(n, 48, feats), enc_b[None], mask)
    act = activation.reshape(tokens, feats)
    share = jnp.stack(
        [jnp.dot(act, dec_w[l], preferred_element_type=F32) for l in range(layers)]
    ).reshape(layers, NZ, rows, width)
    block = (NZ, rows, half)
    sems16 = pltpu.SemaphoreType.DMA((NZ,))
    grads, recon = pl.pallas_call(
        reduce_kernel,
        out_shape=(
            jax.ShapeDtypeStruct((layers, NZ, rows, width), BF16),
            jax.ShapeDtypeStruct((layers, rows, width), BF16),
        ),
        in_specs=vmem(3),
        out_specs=tuple(vmem(2)),
        scratch_shapes=[pltpu.VMEM(block, F32)] * 2
        + [pltpu.VMEM(block, BF16)] * 4
        + [pltpu.SemaphoreType.DMA((2,))] * 2
        + [sems16] * 4
        + sems3
        + GATHER_SEMS,
        compiler_params=params(2),
    )(share, gathered, dec_b[:, None, :])
    recon = lax.dynamic_slice_in_dim(recon, quarter * own, own, 1).transpose(1, 0, 2)
    rg = grads.reshape(layers, tokens, width)
    dec_bias_grad = jnp.sum(rg.astype(F32), axis=1)
    act_part = sum(
        lax.dot_general(rg[l], dec_w[l], (((1,), (1,)), ((), ())), preferred_element_type=F32) for l in range(layers)
    )
    mine = lax.dynamic_index_in_dim(activation, dp, 0, keepdims=False)
    pre_grad = dp_sum(3, pass_grad, act_part.reshape(n, 48, feats), mine).reshape(tokens, feats)
    enc_bias_grad = jnp.sum(pre_grad.astype(F32), axis=0)
    dec_grad = jnp.einsum("tf,ltd->lfd", act, rg, preferred_element_type=F32).astype(BF16)
    enc_grad = jnp.einsum("ltd,tf->ldf", flat, pre_grad, preferred_element_type=F32).astype(BF16)
    return recon, enc_grad, enc_bias_grad, dec_grad, dec_bias_grad


def solution(mesh):
    return jax.shard_map(
        on_device,
        mesh=mesh,
        in_specs=(
            P("feat", None, "dp"),
            P(None, "dp", "feat"),
            P("feat"),
            P(None, "feat", "dp"),
            P(None, "dp"),
            P(),
        ),
        out_specs=(
            P("feat", None, "dp"),
            P(None, "dp", "feat"),
            P("feat"),
            P(None, "feat", "dp"),
            P(None, "dp"),
        ),
        check_vma=False,
    )
```

time: 869 us -> 199 us (0.23)
  waiting for transfers between devices: 671 us -> 0 us
  Pallas kernels: 0 us -> 178 us
  blocking collectives: 146 us -> 0 us
  between operations: 14.5 us -> 0.87 us
    unnamed x5 -> x0, waiting for transfers between devices: 447 us -> none
    pallas_call x0 -> x4, Pallas kernels: none -> 178 us  [the longest x1 81.8 us: on_device(): pl.pallas_call(reduce_kernel, out_shape=(jax.ShapeDtypeStruct((layers, NZ...]
    psum x2 -> x0, blocking collectives: 146 us -> none  [the longest x1 107 us: on_device(): lax.psum(jnp.sum(resid_grad.astype(jnp.float32), axis=0), 'feat')]
    all_gather x2 -> x0, waiting for transfers between devices: 138 us -> none  [the longest x1 129 us: on_device(): gathered = lax.all_gather(residuals, 'feat', axis=0, tiled=True)]
    psum x1 -> x0, waiting for transfers between devices: 86.6 us -> none  [on_device(): pre_act = lax.psum(partial_value, 'dp') + enc_b]
  transfers between devices with their start and end apart: 4 -> 0, of which waited for: 4 -> 0; matrix products, arithmetic and copies ran while one was open for 1% -> 0% of each run, Pallas kernels for 0% -> 0%
where the time goes in v1:
time: 199 us
  Pallas kernels  178 us (89%)
  matrix products  8.56 us (4%)
  local copies, waits for them, and re-layouts  7.66 us (4%)
  other arithmetic  4 us (2%)
    pallas_call x1, Pallas kernels, on_device(): pl.pallas_call(reduce_kernel, out_shape=(jax.ShapeDtypeStruct((layers, NZ...  81.8 us
    pallas_call x1, Pallas kernels, on_device(): pl.pallas_call(gather_kernel, out_shape=jax.ShapeDtypeStruct((layers, NZ,...  62.3 us
    pallas_call x2, Pallas kernels, dp_sum(): pl.pallas_call(functools.partial(dp_sum_kernel, finish, n), out_shape=jax...  33.4 us
    unnamed x16, local copies, waits for them, and re-layouts  7.07 us

profile of v1, /device:TPU:1, one launch (start us, length us, event | category | flops | bytes accessed | tf_op | source)
XLA Modules:
  0.0 198.6 jit_solution(6430430092753028007)
XLA Ops:
  0.7 0.7 copy.33
  1.4 0.2 dynamic_update_slice.3.x_ref
  1.7 62.3 %shard_map.101.resid = bf16[2,16,24,1024]{3,2,1,0:T(8,128)(2,1)S(1)} custom-call(bf16[2,24,1024]{2,1,0:T(8,128)(2,1)S(1)} %dynamic_update_slice.3.x_ref), custom_call_target="tpu_custom_call" | custom-call | tf_op jit(solution)/shard_map/pallas_call | solution.py:296
  64.0 0.0 copy-start.3
  64.0 0.1 fusion.16
  64.1 1.1 copy-done.3
  65.2 0.4 fusion.7
  65.6 0.0 copy-start.1
  65.6 0.4 convolution_add_fusion.1
  66.0 0.1 copy-done.4
  66.1 0.1 copy.24
  66.4 0.6 compare_reduce_fusion
  67.0 0.0 copy-done.1
  67.0 18.3 %shard_map.102 = bf16[8,48,256]{2,1,0:T(8,128)(2,1)S(1)} custom-call(f32[8,48,256]{2,1,0:T(8,128)S(1)} %bitcast.63, f32[1,256]{1,0:T(1,128)S(1)} %bitcast.66, f32[48,256]{1,0:T(8,128)S(1)} %convert_element_type.20.refs_1_), custom_call_target="tpu_custom_call" | custom-call | tf_op jit(solution)/shard_map/pallas_call | solution.py:265
  85.3 1.4 convolution_bitcast_fusion
  86.7 1.4 convolution_bitcast_fusion.1
  88.2 0.0 copy-start.5
  88.2 1.9 pad_maximum_fusion.part
  90.1 0.0 copy-done.5
  90.1 81.8 %shard_map.103 = (bf16[2,16,24,1024]{3,2,1,0:T(8,128)(2,1)S(1)}, bf16[2,24,1024]{2,1,0:T(8,128)(2,1)S(1)}) custom-call(f32[2,16,24,1024]{3,2,1,0:T(8,128)} %pad_maximum_fusion.part, bf16[2,16,24,1024]{3,2,1,0:T(8,128)(2,1)S(1)} %shard_map.101.resid, f32[2,1,1024]{2,1,0:T(1,128)S(1)} %broadcast_in_dim.13.bias), custom_call_target="tpu_custom_call" | custom-call | tf_op jit(solution)/shard_map/pallas_call | solution.py:320
  171.9 1.7 fusion
  173.6 2.3 %copy.29 = bf16[2,256,1024]{2,1,0:T(8,128)(2,1)} copy(bf16[2,256,1024]{1,2,0:T(8,128)(2,1)} %fusion) | data formatting | bytes 2097152
  175.8 0.1 fusion.15
  176.0 1.1 copy-done.2
  177.1 0.4 fusion.4
  177.5 1.2 convolution_add_fusion
  178.6 1.0 copy-done
  179.6 15.1 %shard_map.104 = bf16[8,48,256]{2,1,0:T(8,128)(2,1)S(1)} custom-call(f32[8,48,256]{2,1,0:T(8,128)S(1)} %bitcast.64, bf16[48,256]{1,0:T(8,128)(2,1)S(1)} %dynamic-slice_bitcast_fusion.1.refs_0_), custom_call_target="tpu_custom_call" | custom-call | tf_op jit(solution)/shard_map/pallas_call | solution.py:265
  194.7 1.7 convolution_convert_fusion.1
  196.4 0.6 convert_reduce_fusion.1
  197.1 0.6 copy.28
  197.7 0.9 convert_reduce_fusion
  (13 shorter events, 0.1 us)
Async XLA Ops:
  64.0 1.2 copy-start.3
  65.2 0.9 copy-start.4
  65.6 1.4 copy-start.1
  88.2 1.9 copy-start.5
  175.8 1.2 copy-start.2
  178.6 1.0 copy-start

commit v2 on v1

--- a/solution.py
+++ b/solution.py
@@ -33,7 +33,7 @@
     return (odd * ((i + 1) // 2) + (1 - odd) * (NZ - i // 2)) % NZ
 
 
-def greet_feat():
+def greet_feat(reach):
     y, z, c = place()
     barrier = pltpu.get_barrier_semaphore()
 
@@ -44,11 +44,14 @@
         signal(feat_of(y, (z + i) % NZ, c))
         return carry
 
-    lax.fori_loop(1, NZ, one, 0)
+    far = min(reach, NZ // 2)
+    near = min(reach, NZ // 2 - 1)
+    lax.fori_loop(1, far + 1, one, 0)
+    lax.fori_loop(NZ - near, NZ, one, 0)
     signal(feat_of(1 - y, z, c))
     signal(feat_of(y, z, 1 - c))
     signal(feat_of(1 - y, z, 1 - c))
-    pl.semaphore_wait(barrier, NZ + 2)
+    pl.semaphore_wait(barrier, far + near + 3)
 
 
 def gather_feat(out, sems):
@@ -59,12 +62,9 @@
     def chunk(layer, zz, part):
         return out.at[layer, zz, :, pl.ds(pl.multiple_of(part * half, half), half)]
 
-    def z_copy(s):
-        return rdma(chunk(y, z, c), chunk(y, z, c), zs.at[s], zr.at[s], feat=feat_of(y, (z + s) % NZ, c))
-
-    def z_arrival(s):
-        piece = chunk(y, (z + NZ - s) % NZ, c)
-        return rdma(piece, piece, zs.at[s], zr.at[s], feat=feat_of(y, (z + s) % NZ, c))
+    def z_copy(held, slot, step):
+        piece = chunk(y, (z + NZ - held) % NZ, c)
+        return rdma(piece, piece, zs.at[slot], zr.at[slot], feat=feat_of(y, (z + NZ + step) % NZ, c))
 
     def y_copy(s, layer):
         piece = chunk(layer, (z + NZ - s) % NZ, c)
@@ -78,16 +78,17 @@
         piece = chunk(1 - y, (z + NZ - s) % NZ, part)
         return rdma(piece, piece, ds.at[s], dr.at[s], feat=feat_of(y, z, 1 - c))
 
-    def send(i, carry):
-        z_copy(turn(NZ - i)).start()
-        return carry
-
     def forward(i, carry):
         s = turn(i)
 
         @pl.when(i > 0)
         def _():
-            z_arrival(s).wait_recv()
+            z_copy(s, s, 1).wait_recv()
+
+        @pl.when((i > 0) & (i < 12))
+        def _():
+            step = 4 * (i % 2) - 2
+            z_copy(s, s + step, step).start()
 
         y_copy(s, y).start()
         c_copy(s, c).start()
@@ -103,7 +104,7 @@
     def finish(s, carry):
         @pl.when(s > 0)
         def _():
-            z_copy(s).wait_send()
+            z_copy(0, s, 1).wait_send()
 
         y_copy(s, y).wait_send()
         c_copy(s, c).wait_send()
@@ -112,7 +113,8 @@
         d_copy(s, 1 - c).wait_recv()
         return carry
 
-    lax.fori_loop(1, NZ, send, 0)
+    for step in (1, -1, 2, -2):
+        z_copy(0, step % NZ, step).start()
     lax.fori_loop(0, NZ, forward, 0)
     last = turn(NZ - 1)
     y_copy(last, 1 - y).wait_recv()
@@ -134,7 +136,7 @@
     def cols(part):
         return pl.ds(pl.multiple_of(part * half, half), half)
 
-    greet_feat()
+    greet_feat(2)
     copies = [
         rdma(x_ref.at[yy, :, cols(cc)], got.at[k], gs.at[k], gr.at[k], feat=peer)
         for k, (peer, yy, cc) in enumerate(others(y, z, c))
@@ -158,12 +160,20 @@
     def cols(p):
         return pl.ds(pl.multiple_of(p * half, half), half)
 
-    greet_feat()
+    greet_feat(NZ)
     sibling = feat_of(y, z, 1 - c)
-    first = rdma(part.at[1 - y, :, :, cols(1 - c)], ra, ss.at[0], sr.at[0], feat=sibling)
-    second = rdma(part.at[y, :, :, cols(1 - c)], rb, ss.at[1], sr.at[1], feat=sibling)
-    first.start()
-    second.start()
+
+    def first(zz):
+        return rdma(part.at[1 - y, zz, :, cols(1 - c)], ra.at[zz], ss.at[0, zz], sr.at[0, zz], feat=sibling)
+
+    def second(zz):
+        return rdma(part.at[y, zz, :, cols(1 - c)], rb.at[zz], ss.at[1, zz], sr.at[1, zz], feat=sibling)
+
+    def to_c(i, carry):
+        zz = (z + turn(NZ - 1 - i)) % NZ
+        first(zz).start()
+        second(zz).start()
+        return carry
 
     def y_copy(zz):
         return rdma(sy.at[zz], ry.at[zz], ws.at[zz], wr.at[zz], feat=feat_of(1 - y, z, c))
@@ -173,23 +183,29 @@
 
     def to_y(i, carry):
         zz = (z + turn(NZ - 1 - i)) % NZ
+        first(zz).wait_recv()
         sy[zz] = (part[1 - y, zz, :, cols(c)] + ra[zz]).astype(BF16)
         y_copy(zz).start()
-        return carry
-
-    def to_z(i, carry):
+
+        @pl.when(i > 1)
+        def _():
+            to_z(i - 2)
+
+        return carry
+
+    def to_z(i):
         s = turn(NZ - 1 - i)
         zz = (z + s) % NZ
         y_copy(zz).wait_recv()
+        second(zz).wait_recv()
         sz[s] = (part[y, zz, :, cols(c)] + rb[zz] + ry[zz].astype(F32)).astype(BF16)
         z_copy(s).start()
-        return carry
-
-    first.wait_recv()
+
+    lax.fori_loop(0, NZ, to_c, 0)
     lax.fori_loop(0, NZ, to_y, 0)
-    second.wait_recv()
-    lax.fori_loop(0, NZ - 1, to_z, 0)
+    to_z(NZ - 2)
     y_copy(z).wait_recv()
+    second(z).wait_recv()
     total = part[y, z, :, cols(c)] + rb[z] + ry[z].astype(F32)
 
     def add(i, total):
@@ -201,15 +217,15 @@
     full = total + bias[y, :, cols(c)]
     grad[y, z, :, cols(c)] = ((full - resid[y, z, :, cols(c)].astype(F32)) * 0.25).astype(BF16)
     recon[y, :, cols(c)] = full.astype(BF16)
-    gather_feat(grad, sems)
     mine = recon.at[y, :, cols(c)]
     copies = [rdma(mine, mine, gs.at[k], gr.at[k], feat=peer) for k, (peer, _, _) in enumerate(others(y, z, c))]
     for copy in copies:
         copy.start()
-    first.wait_send()
-    second.wait_send()
+    gather_feat(grad, sems)
 
     def drain(i, carry):
+        first(i).wait_send()
+        second(i).wait_send()
         y_copy(i).wait_send()
 
         @pl.when(i > 0)
@@ -327,7 +343,7 @@
         out_specs=tuple(vmem(2)),
         scratch_shapes=[pltpu.VMEM(block, F32)] * 2
         + [pltpu.VMEM(block, BF16)] * 4
-        + [pltpu.SemaphoreType.DMA((2,))] * 2
+        + [pltpu.SemaphoreType.DMA((2, NZ))] * 2
         + [sems16] * 4
         + sems3
         + GATHER_SEMS,

time: 199 us -> 162 us (0.81)
  Pallas kernels: 178 us -> 140 us
    pallas_call x1, Pallas kernels: 81.8 us -> 62.7 us  [on_device(): pl.pallas_call(reduce_kernel, out_shape=(jax.ShapeDtypeStruct((layers, NZ...]
    pallas_call x1, Pallas kernels: 62.3 us -> 43.6 us  [on_device(): pl.pallas_call(gather_kernel, out_shape=jax.ShapeDtypeStruct((layers, NZ,...]
where the time goes in v2:
time: 162 us; the launch traced here: 161 us
  Pallas kernels  140 us (86%)
  matrix products  8.57 us (5%)
  local copies, waits for them, and re-layouts  7.66 us (5%)
  other arithmetic  4 us (2%)
    pallas_call x1, Pallas kernels, on_device(): pl.pallas_call(reduce_kernel, out_shape=(jax.ShapeDtypeStruct((layers, NZ...  62.7 us
    pallas_call x1, Pallas kernels, on_device(): pl.pallas_call(gather_kernel, out_shape=jax.ShapeDtypeStruct((layers, NZ,...  43.6 us
    pallas_call x2, Pallas kernels, dp_sum(): pl.pallas_call(functools.partial(dp_sum_kernel, finish, n), out_shape=jax...  33.5 us
    unnamed x16, local copies, waits for them, and re-layouts  7.07 us

profile of v2, /device:TPU:1, one launch (start us, length us, event | category | flops | bytes accessed | tf_op | source)
XLA Modules:
  0.0 161.0 jit_solution(9880647523348602295)
XLA Ops:
  0.7 0.7 copy.33
  1.4 0.2 dynamic_update_slice.3.x_ref
  1.7 43.6 %shard_map.101.resid = bf16[2,16,24,1024]{3,2,1,0:T(8,128)(2,1)S(1)} custom-call(bf16[2,24,1024]{2,1,0:T(8,128)(2,1)S(1)} %dynamic_update_slice.3.x_ref), custom_call_target="tpu_custom_call" | custom-call | tf_op jit(solution)/shard_map/pallas_call | solution.py:312
  45.3 0.0 copy-start.3
  45.3 0.1 fusion.16
  45.4 1.1 copy-done.3
  46.5 0.4 fusion.7
  46.9 0.0 copy-start.1
  46.9 0.4 convolution_add_fusion.1
  47.3 0.1 copy-done.4
  47.4 0.1 copy.24
  47.6 0.6 compare_reduce_fusion
  48.2 0.0 copy-done.1
  48.3 18.0 %shard_map.102 = bf16[8,48,256]{2,1,0:T(8,128)(2,1)S(1)} custom-call(f32[8,48,256]{2,1,0:T(8,128)S(1)} %bitcast.63, f32[1,256]{1,0:T(1,128)S(1)} %bitcast.66, f32[48,256]{1,0:T(8,128)S(1)} %convert_element_type.20.refs_1_), custom_call_target="tpu_custom_call" | custom-call | tf_op jit(solution)/shard_map/pallas_call | solution.py:281
  66.3 1.4 convolution_bitcast_fusion
  67.7 1.4 convolution_bitcast_fusion.1
  69.1 0.0 copy-start.5
  69.1 1.9 %pad_maximum_fusion.part = f32[2,16,24,1024]{3,2,1,0:T(8,128)} fusion(f32[1,16,24,1024]{3,2,1,0:T(8,128)S(1)} %convolution_bitcast_fusion, f32[1,16,24,1024]{3,2,1,0:T(8,128)S(1)} %convolution_bitcast_fusion.1), kind=kLoop, calls=%fused_computation | loop fusion | flops 786432 | bytes 6291456 | tf_op jit(solution)/shard_map/stack | solution.py:331
  71.0 0.0 copy-done.5
  71.0 62.7 %shard_map.103 = (bf16[2,16,24,1024]{3,2,1,0:T(8,128)(2,1)S(1)}, bf16[2,24,1024]{2,1,0:T(8,128)(2,1)S(1)}) custom-call(f32[2,16,24,1024]{3,2,1,0:T(8,128)} %pad_maximum_fusion.part, bf16[2,16,24,1024]{3,2,1,0:T(8,128)(2,1)S(1)} %shard_map.101.resid, f32[2,1,1024]{2,1,0:T(1,128)S(1)} %broadcast_in_dim.13.bias), custom_call_target="tpu_custom_call" | custom-call | tf_op jit(solution)/shard_map/pallas_call | solution.py:336
  133.8 1.7 %fusion = bf16[2,256,1024]{1,2,0:T(8,128)(2,1)} fusion(bf16[2,384,1024]{2,1,0:T(8,128)(2,1)S(1)} %bitcast.59, bf16[384,256,1]{1,0,2:T(8,128)(2,1)S(1)} %bitcast.62), kind=kOutput, calls=%fused_computation.7 | convolution fusion | flops 403177472 | bytes 2818048 | tf_op jit(solution)/shard_map/tf,ltd->lfd/dot_general | solution.py:361
  135.5 2.3 %copy.29 = bf16[2,256,1024]{2,1,0:T(8,128)(2,1)} copy(bf16[2,256,1024]{1,2,0:T(8,128)(2,1)} %fusion) | data formatting | bytes 2097152
  137.7 0.1 fusion.15
  137.9 1.1 copy-done.2
  139.0 0.4 fusion.4
  139.4 1.2 convolution_add_fusion
  140.5 1.0 copy-done
  141.5 15.5 %shard_map.104 = bf16[8,48,256]{2,1,0:T(8,128)(2,1)S(1)} custom-call(f32[8,48,256]{2,1,0:T(8,128)S(1)} %bitcast.64, bf16[48,256]{1,0:T(8,128)(2,1)S(1)} %dynamic-slice_bitcast_fusion.1.refs_0_), custom_call_target="tpu_custom_call" | custom-call | tf_op jit(solution)/shard_map/pallas_call | solution.py:281
  157.1 1.7 %convolution_convert_fusion.1 = bf16[2,1024,256]{2,1,0:T(8,128)(2,1)} fusion(bf16[2,384,1024]{2,1,0:T(8,128)(2,1)S(1)} %bitcast.58, bf16[384,256,1]{1,0,2:T(8,128)(2,1)S(1)} %bitcast.65), kind=kOutput, calls=%fused_computation.4 | convolution fusion | flops 403177472 | bytes 2818048 | tf_op jit(solution)/shard_map/ltd,tf->ldf/dot_general | solution.py:362
  158.8 0.6 convert_reduce_fusion.1
  159.4 0.6 copy.28
  160.1 0.9 convert_reduce_fusion
  (13 shorter events, 0.1 us)
Async XLA Ops:
  45.3 1.2 copy-start.3
  46.5 0.9 copy-start.4
  46.9 1.4 copy-start.1
  69.1 1.9 %copy-start.5 = (f32[2,1024]{1,0:T(2,128)S(1)}, f32[2,1024]{1,0:T(2,128)}, u32[]{:S(2)}) copy-start(f32[2,1024]{1,0:T(2,128)} %param.10) | copy-start | bytes 24580
  137.7 1.2 copy-start.2
  140.5 1.0 copy-start

commit v3 on v2

--- a/solution.py
+++ b/solution.py
@@ -51,7 +51,11 @@
     signal(feat_of(1 - y, z, c))
     signal(feat_of(y, z, 1 - c))
     signal(feat_of(1 - y, z, 1 - c))
-    pl.semaphore_wait(barrier, far + near + 3)
+    return far + near + 3
+
+
+def await_greetings(count):
+    pl.semaphore_wait(pltpu.get_barrier_semaphore(), count)
 
 
 def gather_feat(out, sems):
@@ -136,7 +140,7 @@
     def cols(part):
         return pl.ds(pl.multiple_of(part * half, half), half)
 
-    greet_feat(2)
+    await_greetings(greet_feat(2))
     copies = [
         rdma(x_ref.at[yy, :, cols(cc)], got.at[k], gs.at[k], gr.at[k], feat=peer)
         for k, (peer, yy, cc) in enumerate(others(y, z, c))
@@ -153,14 +157,18 @@
         copy.wait_send()
 
 
-def reduce_kernel(part, resid, bias, grad, recon, ra, rb, ry, rz, sy, sz, ss, sr, ws, wr, vs, vr, gs, gr, *sems):
+def reduce_kernel(act, dec, resid, bias, grad, recon, part, ra, rb, ry, rz, sy, sz, ss, sr, ws, wr, vs, vr, gs, gr, *sems):
     y, z, c = place()
     half = part.shape[3] // 2
 
     def cols(p):
         return pl.ds(pl.multiple_of(p * half, half), half)
 
-    greet_feat(NZ)
+    count = greet_feat(NZ)
+    for layer, p in ((1 - y, 1 - c), (y, 1 - c), (1 - y, c), (y, c)):
+        product = jnp.dot(act[...], dec[layer, :, cols(p)], preferred_element_type=F32)
+        part[layer, :, :, cols(p)] = product.reshape(NZ, part.shape[2], half)
+    await_greetings(count)
     sibling = feat_of(y, z, 1 - c)
 
     def first(zz):
@@ -241,23 +249,27 @@
         rdma(piece, piece, gs.at[k], gr.at[k], feat=peer).wait_recv()
 
 
-def dp_sum_kernel(finish, n, part, *refs):
-    extra, (out, got, ps, pr, qs, qr) = refs[:-6], refs[-6:]
+def greet_dp(n):
     me = lax.axis_index("dp")
     barrier = pltpu.get_barrier_semaphore()
     for s in range(1, n):
         pl.semaphore_signal(barrier, inc=1, device_id={"dp": (me + s) % n}, device_id_type=MESH)
-    pl.semaphore_wait(barrier, n - 1)
+
+
+def dp_sum(n, part, out, got, ps, pr, qs, qr, finish, meanwhile=None):
+    me = lax.axis_index("dp")
     copies = [
         rdma(part.at[(me + s) % n], got.at[s], ps.at[s], pr.at[s], dp=(me + s) % n) for s in range(1, n)
     ]
     for copy in copies:
         copy.start()
+    if meanwhile is not None:
+        meanwhile()
     total = part[me]
     for s, copy in enumerate(copies, 1):
         copy.wait_recv()
         total = total + got[s]
-    out[me] = finish(total, *[ref[...] for ref in extra])
+    out[me] = finish(total, me)
     backs = [rdma(out.at[me], out.at[me], qs.at[s], qr.at[s], dp=(me + s) % n) for s in range(1, n)]
     for back in backs:
         back.start()
@@ -268,6 +280,41 @@
         rdma(piece, piece, qs.at[s], qr.at[s], dp=(me + s) % n).wait_recv()
 
 
+def encode_kernel(n, x, w, bias, mask, out, part, *rest):
+    greet_dp(n)
+    pre = jnp.dot(x[0], w[0], preferred_element_type=F32)
+    for l in range(1, x.shape[0]):
+        pre = pre + jnp.dot(x[l], w[l], preferred_element_type=F32)
+    part[...] = pre.reshape(part.shape)
+    await_greetings(n - 1)
+
+    def activate(total, me):
+        return (jnp.maximum(total + bias[...], 0.0) * mask[...]).astype(BF16)
+
+    dp_sum(n, part, out, *rest, activate)
+
+
+def backward_kernel(n, grad, dec, act, out, dec_grad, part, *rest):
+    greet_dp(n)
+    contract_last = (((1,), (1,)), ((), ()))
+    back = lax.dot_general(grad[0], dec[0], contract_last, preferred_element_type=F32)
+    for l in range(1, grad.shape[0]):
+        back = back + lax.dot_general(grad[l], dec[l], contract_last, preferred_element_type=F32)
+    part[...] = back.reshape(part.shape)
+    await_greetings(n - 1)
+
+    def decoder_grad():
+        for l in range(grad.shape[0]):
+            dec_grad[l] = lax.dot_general(
+                act[...].reshape(-1, act.shape[2]), grad[l], (((0,), (0,)), ((), ())), preferred_element_type=F32
+            ).astype(BF16)
+
+    def pass_grad(total, me):
+        return jnp.where(act[me].astype(F32) > 0, total, 0.0).astype(BF16)
+
+    dp_sum(n, part, out, *rest, pass_grad, decoder_grad)
+
+
 def vmem(count):
     return [pl.BlockSpec(memory_space=pltpu.VMEM)] * count
 
@@ -276,24 +323,8 @@
     return pltpu.CompilerParams(collective_id=number, has_side_effects=True, vmem_limit_bytes=48 * 1024 * 1024)
 
 
-def dp_sum(number, finish, part, *extra):
-    n, rows, feats = part.shape
-    return pl.pallas_call(
-        functools.partial(dp_sum_kernel, finish, n),
-        out_shape=jax.ShapeDtypeStruct(part.shape, BF16),
-        in_specs=vmem(1 + len(extra)),
-        out_specs=vmem(1)[0],
-        scratch_shapes=[pltpu.VMEM(part.shape, F32)] + [pltpu.SemaphoreType.DMA((n,))] * 4,
-        compiler_params=params(number),
-    )(part, *extra)
-
-
-def activate(total, bias, mask):
-    return (jnp.maximum(total + bias, 0.0) * mask).astype(BF16)
-
-
-def pass_grad(total, activation):
-    return jnp.where(activation.astype(F32) > 0, total, 0.0).astype(BF16)
+def dp_scratch(block):
+    return [pltpu.VMEM(block, F32)] * 2 + [pltpu.SemaphoreType.DMA((block[0],))] * 4
 
 
 def on_device(residuals, enc_w, enc_b, dec_w, dec_b, active):
@@ -318,19 +349,20 @@
         compiler_params=params(0),
     )(spread)
     flat = gathered.reshape(layers, tokens, width)
-    partial_value = jnp.dot(flat[0], enc_w[0], preferred_element_type=F32) + jnp.dot(
-        flat[1], enc_w[1], preferred_element_type=F32
-    )
     n = tokens // 48
+    dp_block = (n, 48, feats)
     table = active.reshape(2, NZ, 2, own, -1).transpose(1, 0, 2, 3, 4).reshape(tokens, -1)
     table = lax.dynamic_slice_in_dim(table, dp * 48, 48, 0)
     columns = feat * feats + lax.iota(jnp.int32, feats)
     mask = jnp.any(table[:, :, None] == columns[None, None, :], axis=1).astype(F32)
-    activation = dp_sum(1, activate, partial_value.reshape(n, 48, feats), enc_b[None], mask)
-    act = activation.reshape(tokens, feats)
-    share = jnp.stack(
-        [jnp.dot(act, dec_w[l], preferred_element_type=F32) for l in range(layers)]
-    ).reshape(layers, NZ, rows, width)
+    activation = pl.pallas_call(
+        functools.partial(encode_kernel, n),
+        out_shape=jax.ShapeDtypeStruct(dp_block, BF16),
+        in_specs=vmem(4),
+        out_specs=vmem(1)[0],
+        scratch_shapes=dp_scratch(dp_block),
+        compiler_params=params(1),
+    )(flat, enc_w, enc_b[None], mask)
     block = (NZ, rows, half)
     sems16 = pltpu.SemaphoreType.DMA((NZ,))
     grads, recon = pl.pallas_call(
@@ -339,26 +371,30 @@
             jax.ShapeDtypeStruct((layers, NZ, rows, width), BF16),
             jax.ShapeDtypeStruct((layers, rows, width), BF16),
         ),
-        in_specs=vmem(3),
+        in_specs=vmem(4),
         out_specs=tuple(vmem(2)),
-        scratch_shapes=[pltpu.VMEM(block, F32)] * 2
+        scratch_shapes=[pltpu.VMEM((layers, NZ, rows, width), F32)]
+        + [pltpu.VMEM(block, F32)] * 2
         + [pltpu.VMEM(block, BF16)] * 4
         + [pltpu.SemaphoreType.DMA((2, NZ))] * 2
         + [sems16] * 4
         + sems3
         + GATHER_SEMS,
         compiler_params=params(2),
-    )(share, gathered, dec_b[:, None, :])
+    )(activation.reshape(tokens, feats), dec_w, gathered, dec_b[:, None, :])
     recon = lax.dynamic_slice_in_dim(recon, quarter * own, own, 1).transpose(1, 0, 2)
     rg = grads.reshape(layers, tokens, width)
     dec_bias_grad = jnp.sum(rg.astype(F32), axis=1)
-    act_part = sum(
-        lax.dot_general(rg[l], dec_w[l], (((1,), (1,)), ((), ())), preferred_element_type=F32) for l in range(layers)
-    )
-    mine = lax.dynamic_index_in_dim(activation, dp, 0, keepdims=False)
-    pre_grad = dp_sum(3, pass_grad, act_part.reshape(n, 48, feats), mine).reshape(tokens, feats)
+    pre_grad, dec_grad = pl.pallas_call(
+        functools.partial(backward_kernel, n),
+        out_shape=(jax.ShapeDtypeStruct(dp_block, BF16), jax.ShapeDtypeStruct(dec_w.shape, BF16)),
+        in_specs=vmem(3),
+        out_specs=tuple(vmem(2)),
+        scratch_shapes=dp_scratch(dp_block),
+        compiler_params=params(3),
+    )(rg, dec_w, activation)
+    pre_grad = pre_grad.reshape(tokens, feats)
     enc_bias_grad = jnp.sum(pre_grad.astype(F32), axis=0)
-    dec_grad = jnp.einsum("tf,ltd->lfd", act, rg, preferred_element_type=F32).astype(BF16)
     enc_grad = jnp.einsum("ltd,tf->ldf", flat, pre_grad, preferred_element_type=F32).astype(BF16)
     return recon, enc_grad, enc_bias_grad, dec_grad, dec_bias_grad
 

time: 162 us -> 148 us (0.914)
  matrix products: 8.57 us -> 1.72 us
  local copies, waits for them, and re-layouts: 7.66 us -> 4.44 us
  Pallas kernels: 140 us -> 138 us
  other arithmetic: 4 us -> 2.12 us
    dot_general x7 -> x0, matrix products: 6.85 us -> none  [the longest x2 2.83 us: on_device(): jnp.dot(act, dec_w[l], preferred_element_type=F32)]
    unnamed x16 -> x10, local copies, waits for them, and re-layouts: 7.07 us -> 3.39 us
    another operation x1 -> x0, other arithmetic: 1.88 us -> none  [on_device(): jnp.stack([jnp.dot(act, dec_w[l], preferred_element_type=F32) for l in ra...]
    pallas_call x1, Pallas kernels: 62.7 us -> 61.1 us  [on_device(): pl.pallas_call(reduce_kernel, out_shape=(jax.ShapeDtypeStruct((layers, NZ...]
where the time goes in v3:
time: 148 us; the launch traced here: 147 us
  Pallas kernels  138 us (93%)
  local copies, waits for them, and re-layouts  4.44 us (3%)
  other arithmetic  2.12 us (1%)
  matrix products  1.72 us (1%)
    pallas_call x1, Pallas kernels, on_device(): pl.pallas_call(reduce_kernel, out_shape=(jax.ShapeDtypeStruct((layers, NZ...  61.1 us
    pallas_call x1, Pallas kernels, on_device(): pl.pallas_call(gather_kernel, out_shape=jax.ShapeDtypeStruct((layers, NZ,...  43.6 us
    pallas_call x1, Pallas kernels, on_device(): pl.pallas_call(functools.partial(encode_kernel, n), out_shape=jax.ShapeDt...  18.1 us
    pallas_call x1, Pallas kernels, on_device(): pl.pallas_call(functools.partial(backward_kernel, n), out_shape=(jax.Shap...  15.1 us
    unnamed x10, local copies, waits for them, and re-layouts  3.39 us

profile of v3, /device:TPU:1, one launch (start us, length us, event | category | flops | bytes accessed | tf_op | source)
XLA Modules:
  0.0 147.0 jit_solution(13617574578397663759)
XLA Ops:
  0.7 0.7 broadcast_in_dim.13.bias
  1.4 0.7 copy.26
  2.1 0.2 dynamic_update_slice.3.x_ref
  2.4 1.0 copy.20
  3.4 0.0 copy-start.1
  3.4 0.0 copy-start.2
  3.5 0.6 compare_reduce_fusion
  4.1 43.6 %shard_map.101.resid = bf16[2,16,24,1024]{3,2,1,0:T(8,128)(2,1)S(1)} custom-call(bf16[2,24,1024]{2,1,0:T(8,128)(2,1)S(1)} %dynamic_update_slice.3.x_ref), custom_call_target="tpu_custom_call" | custom-call | tf_op jit(solution)/shard_map/pallas_call | solution.py:343
  47.7 0.0 copy-start
  47.8 0.0 copy-done.1
  47.8 0.0 copy-done.2
  47.8 18.1 %shard_map.102.act = bf16[8,48,256]{2,1,0:T(8,128)(2,1)S(1)} custom-call(bf16[2,384,1024]{2,1,0:T(8,128)(2,1)S(1)} %bitcast.15, bf16[2,1024,256]{2,1,0:T(8,128)(2,1)S(1)} %copy-done.1, f32[1,256]{1,0:T(1,128)S(1)} %bitcast.20, f32[48,256]{1,0:T(8,128)S(1)} %convert_element_type.14.mask), custom_call_target="tpu_custom_call" | custom-call | tf_op jit(solution)/shard_map/pallas_call | solution.py:358
  65.9 0.0 copy-done
  65.9 61.1 %shard_map.103 = (bf16[2,16,24,1024]{3,2,1,0:T(8,128)(2,1)S(1)}, bf16[2,24,1024]{2,1,0:T(8,128)(2,1)S(1)}) custom-call(bf16[384,256]{1,0:T(8,128)(2,1)S(1)} %bitcast.18, bf16[2,256,1024]{2,1,0:T(8,128)(2,1)S(1)} %copy-done, bf16[2,16,24,1024]{3,2,1,0:T(8,128)(2,1)S(1)} %shard_map.101.resid, f32[2,1,1024]{2,1,0:T(1,128)S(1)} %broadcast_in_dim.13.bias), custom_call_target="tpu_custom_call" | custom-call | tf_op jit(solution)/shard_map/pallas_call | solution.py:368
  127.1 0.6 copy.23
  127.7 0.9 convert_reduce_fusion
  128.6 15.1 %shard_map.104 = (bf16[8,48,256]{2,1,0:T(8,128)(2,1)S(1)}, bf16[2,256,1024]{2,1,0:T(8,128)(2,1)S(1)}) custom-call(bf16[2,384,1024]{2,1,0:T(8,128)(2,1)S(1)} %bitcast.17, bf16[2,256,1024]{2,1,0:T(8,128)(2,1)S(1)} %copy-done, bf16[8,48,256]{2,1,0:T(8,128)(2,1)S(1)} %shard_map.102.act), custom_call_target="tpu_custom_call" | custom-call | tf_op jit(solution)/shard_map/pallas_call | solution.py:388
  143.7 1.7 %convolution_convert_fusion = bf16[2,1024,256]{2,1,0:T(8,128)(2,1)} fusion(bf16[2,384,1024]{2,1,0:T(8,128)(2,1)S(1)} %bitcast.16, bf16[384,256,1]{1,0,2:T(8,128)(2,1)S(1)} %bitcast.19), kind=kOutput, calls=%fused_computation.2 | convolution fusion | flops 403177472 | bytes 2818048 | tf_op jit(solution)/shard_map/ltd,tf->ldf/dot_general | solution.py:398
  145.5 0.6 convert_reduce_fusion.1
  146.1 1.0 copy.29
  (8 shorter events, 0.1 us)
Async XLA Ops:
  3.4 44.4 %copy-start.1 = (bf16[2,1024,256]{2,1,0:T(8,128)(2,1)S(1)}, bf16[2,1024,256]{2,1,0:T(8,128)(2,1)}, u32[]{:S(2)}) copy-start(bf16[2,1024,256]{2,1,0:T(8,128)(2,1)} %w.1) | copy-start | bytes 3145732
  3.4 44.4 %copy-start.2 = (f32[256]{0:T(256)S(1)}, f32[256]{0:T(256)}, u32[]{:S(2)}) copy-start(f32[256]{0:T(256)} %param.8) | copy-start | bytes 3076
  47.7 18.2 %copy-start = (bf16[2,256,1024]{2,1,0:T(8,128)(2,1)S(1)}, bf16[2,256,1024]{2,1,0:T(8,128)(2,1)}, u32[]{:S(2)}) copy-start(bf16[2,256,1024]{2,1,0:T(8,128)(2,1)} %dec.3) | copy-start | bytes 3145732

commit v4 on v3

--- a/solution.py
+++ b/solution.py
@@ -9,6 +9,7 @@
 
 MESH = pl.DeviceIdType.MESH
 NZ = 16
+LAG = 5
 F32 = jnp.float32
 BF16 = jnp.bfloat16
 
@@ -97,12 +98,16 @@
         y_copy(s, y).start()
         c_copy(s, c).start()
 
-        @pl.when(i > 0)
-        def _():
-            before = turn(i - 1)
-            y_copy(before, 1 - y).wait_recv()
-            d_copy(before, c).start()
-
+        @pl.when(i >= LAG)
+        def _():
+            pass_on(i - LAG, 0)
+
+        return carry
+
+    def pass_on(i, carry):
+        s = turn(i)
+        y_copy(s, 1 - y).wait_recv()
+        d_copy(s, c).start()
         return carry
 
     def finish(s, carry):
@@ -120,9 +125,7 @@
     for step in (1, -1, 2, -2):
         z_copy(0, step % NZ, step).start()
     lax.fori_loop(0, NZ, forward, 0)
-    last = turn(NZ - 1)
-    y_copy(last, 1 - y).wait_recv()
-    d_copy(last, c).start()
+    lax.fori_loop(NZ - LAG, NZ, pass_on, 0)
     lax.fori_loop(0, NZ, finish, 0)
 
 
@@ -195,23 +198,24 @@
         sy[zz] = (part[1 - y, zz, :, cols(c)] + ra[zz]).astype(BF16)
         y_copy(zz).start()
 
-        @pl.when(i > 1)
-        def _():
-            to_z(i - 2)
-
-        return carry
-
-    def to_z(i):
+        @pl.when(i >= LAG)
+        def _():
+            to_z(i - LAG, 0)
+
+        return carry
+
+    def to_z(i, carry):
         s = turn(NZ - 1 - i)
         zz = (z + s) % NZ
         y_copy(zz).wait_recv()
         second(zz).wait_recv()
         sz[s] = (part[y, zz, :, cols(c)] + rb[zz] + ry[zz].astype(F32)).astype(BF16)
         z_copy(s).start()
+        return carry
 
     lax.fori_loop(0, NZ, to_c, 0)
     lax.fori_loop(0, NZ, to_y, 0)
-    to_z(NZ - 2)
+    lax.fori_loop(NZ - LAG, NZ - 1, to_z, 0)
     y_copy(z).wait_recv()
     second(z).wait_recv()
     total = part[y, z, :, cols(c)] + rb[z] + ry[z].astype(F32)

time: 148 us -> 133 us (0.90)
  Pallas kernels: 138 us -> 124 us
    pallas_call x1, Pallas kernels: 43.6 us -> 35.2 us  [on_device(): pl.pallas_call(gather_kernel, out_shape=jax.ShapeDtypeStruct((layers, NZ,...]
    pallas_call x1, Pallas kernels: 61.1 us -> 55.7 us  [on_device(): pl.pallas_call(reduce_kernel, out_shape=(jax.ShapeDtypeStruct((layers, NZ...]
where the time goes in v4:
time: 133 us
  Pallas kernels  124 us (93%)
  local copies, waits for them, and re-layouts  4.44 us (3%)
  other arithmetic  2.12 us (2%)
  matrix products  1.72 us (1%)
    pallas_call x1, Pallas kernels, on_device(): pl.pallas_call(reduce_kernel, out_shape=(jax.ShapeDtypeStruct((layers, NZ...  55.7 us
    pallas_call x1, Pallas kernels, on_device(): pl.pallas_call(gather_kernel, out_shape=jax.ShapeDtypeStruct((layers, NZ,...  35.2 us
    pallas_call x1, Pallas kernels, on_device(): pl.pallas_call(functools.partial(encode_kernel, n), out_shape=jax.ShapeDt...  18.2 us
    pallas_call x1, Pallas kernels, on_device(): pl.pallas_call(functools.partial(backward_kernel, n), out_shape=(jax.Shap...  14.7 us
    unnamed x10, local copies, waits for them, and re-layouts  3.39 us

profile of v4, /device:TPU:1, one launch (start us, length us, event | category | flops | bytes accessed | tf_op | source)
XLA Modules:
  0.0 132.9 jit_solution(420073774173062185)
XLA Ops:
  0.7 0.7 broadcast_in_dim.13.bias
  1.4 0.7 copy.26
  2.1 0.2 dynamic_update_slice.3.x_ref
  2.4 1.0 copy.20
  3.4 0.0 copy-start.1
  3.4 0.0 copy-start.2
  3.5 0.6 compare_reduce_fusion
  4.1 35.2 %shard_map.101.resid = bf16[2,16,24,1024]{3,2,1,0:T(8,128)(2,1)S(1)} custom-call(bf16[2,24,1024]{2,1,0:T(8,128)(2,1)S(1)} %dynamic_update_slice.3.x_ref), custom_call_target="tpu_custom_call" | custom-call | tf_op jit(solution)/shard_map/pallas_call | solution.py:347
  39.3 0.0 copy-start
  39.3 0.0 copy-done.1
  39.3 0.0 copy-done.2
  39.4 18.2 %shard_map.102.act = bf16[8,48,256]{2,1,0:T(8,128)(2,1)S(1)} custom-call(bf16[2,384,1024]{2,1,0:T(8,128)(2,1)S(1)} %bitcast.15, bf16[2,1024,256]{2,1,0:T(8,128)(2,1)S(1)} %copy-done.1, f32[1,256]{1,0:T(1,128)S(1)} %bitcast.20, f32[48,256]{1,0:T(8,128)S(1)} %convert_element_type.14.mask), custom_call_target="tpu_custom_call" | custom-call | tf_op jit(solution)/shard_map/pallas_call | solution.py:362
  57.5 0.0 copy-done
  57.6 55.7 %shard_map.103 = (bf16[2,16,24,1024]{3,2,1,0:T(8,128)(2,1)S(1)}, bf16[2,24,1024]{2,1,0:T(8,128)(2,1)S(1)}) custom-call(bf16[384,256]{1,0:T(8,128)(2,1)S(1)} %bitcast.18, bf16[2,256,1024]{2,1,0:T(8,128)(2,1)S(1)} %copy-done, bf16[2,16,24,1024]{3,2,1,0:T(8,128)(2,1)S(1)} %shard_map.101.resid, f32[2,1,1024]{2,1,0:T(1,128)S(1)} %broadcast_in_dim.13.bias), custom_call_target="tpu_custom_call" | custom-call | tf_op jit(solution)/shard_map/pallas_call | solution.py:372
  113.3 0.6 copy.23
  113.9 0.9 convert_reduce_fusion
  114.8 14.7 %shard_map.104 = (bf16[8,48,256]{2,1,0:T(8,128)(2,1)S(1)}, bf16[2,256,1024]{2,1,0:T(8,128)(2,1)S(1)}) custom-call(bf16[2,384,1024]{2,1,0:T(8,128)(2,1)S(1)} %bitcast.17, bf16[2,256,1024]{2,1,0:T(8,128)(2,1)S(1)} %copy-done, bf16[8,48,256]{2,1,0:T(8,128)(2,1)S(1)} %shard_map.102.act), custom_call_target="tpu_custom_call" | custom-call | tf_op jit(solution)/shard_map/pallas_call | solution.py:392
  129.5 1.7 %convolution_convert_fusion = bf16[2,1024,256]{2,1,0:T(8,128)(2,1)} fusion(bf16[2,384,1024]{2,1,0:T(8,128)(2,1)S(1)} %bitcast.16, bf16[384,256,1]{1,0,2:T(8,128)(2,1)S(1)} %bitcast.19), kind=kOutput, calls=%fused_computation.2 | convolution fusion | flops 403177472 | bytes 2818048 | tf_op jit(solution)/shard_map/ltd,tf->ldf/dot_general | solution.py:402
  131.3 0.6 convert_reduce_fusion.1
  131.9 1.0 copy.29
  (8 shorter events, 0.1 us)
Async XLA Ops:
  3.4 35.9 %copy-start.1 = (bf16[2,1024,256]{2,1,0:T(8,128)(2,1)S(1)}, bf16[2,1024,256]{2,1,0:T(8,128)(2,1)}, u32[]{:S(2)}) copy-start(bf16[2,1024,256]{2,1,0:T(8,128)(2,1)} %w.1) | copy-start | bytes 3145732
  3.4 35.9 %copy-start.2 = (f32[256]{0:T(256)S(1)}, f32[256]{0:T(256)}, u32[]{:S(2)}) copy-start(f32[256]{0:T(256)} %param.8) | copy-start | bytes 3076
  39.3 18.2 %copy-start = (bf16[2,256,1024]{2,1,0:T(8,128)(2,1)S(1)}, bf16[2,256,1024]{2,1,0:T(8,128)(2,1)}, u32[]{:S(2)}) copy-start(bf16[2,256,1024]{2,1,0:T(8,128)(2,1)} %dec.3) | copy-start | bytes 3145732

commit v5 on v4

--- a/solution.py
+++ b/solution.py
@@ -9,7 +9,7 @@
 
 MESH = pl.DeviceIdType.MESH
 NZ = 16
-LAG = 5
+LAG = 8
 F32 = jnp.float32
 BF16 = jnp.bfloat16
 

time: 133 us -> 133 us (level)
  no operation moved by 1% of the time
where the time goes in v5:
time: 133 us
  Pallas kernels  124 us (93%)
  local copies, waits for them, and re-layouts  4.44 us (3%)
  other arithmetic  2.12 us (2%)
  matrix products  1.73 us (1%)
    pallas_call x1, Pallas kernels, on_device(): pl.pallas_call(reduce_kernel, out_shape=(jax.ShapeDtypeStruct((layers, NZ...  55.9 us
    pallas_call x1, Pallas kernels, on_device(): pl.pallas_call(gather_kernel, out_shape=jax.ShapeDtypeStruct((layers, NZ,...  35.2 us
    pallas_call x1, Pallas kernels, on_device(): pl.pallas_call(functools.partial(encode_kernel, n), out_shape=jax.ShapeDt...  18.2 us
    pallas_call x1, Pallas kernels, on_device(): pl.pallas_call(functools.partial(backward_kernel, n), out_shape=(jax.Shap...  14.7 us
    unnamed x10, local copies, waits for them, and re-layouts  3.39 us

profile of v5, /device:TPU:1, one launch (start us, length us, event | category | flops | bytes accessed | tf_op | source)
XLA Modules:
  0.0 133.1 jit_solution(1217606556909101680)
XLA Ops:
  0.7 0.7 broadcast_in_dim.13.bias
  1.4 0.7 copy.26
  2.1 0.2 dynamic_update_slice.3.x_ref
  2.4 1.0 copy.20
  3.4 0.0 copy-start.1
  3.4 0.0 copy-start.2
  3.5 0.6 compare_reduce_fusion
  4.1 35.2 %shard_map.101.resid = bf16[2,16,24,1024]{3,2,1,0:T(8,128)(2,1)S(1)} custom-call(bf16[2,24,1024]{2,1,0:T(8,128)(2,1)S(1)} %dynamic_update_slice.3.x_ref), custom_call_target="tpu_custom_call" | custom-call | tf_op jit(solution)/shard_map/pallas_call | solution.py:347
  39.3 0.0 copy-start
  39.3 0.0 copy-done.1
  39.3 0.0 copy-done.2
  39.3 18.2 %shard_map.102.act = bf16[8,48,256]{2,1,0:T(8,128)(2,1)S(1)} custom-call(bf16[2,384,1024]{2,1,0:T(8,128)(2,1)S(1)} %bitcast.15, bf16[2,1024,256]{2,1,0:T(8,128)(2,1)S(1)} %copy-done.1, f32[1,256]{1,0:T(1,128)S(1)} %bitcast.20, f32[48,256]{1,0:T(8,128)S(1)} %convert_element_type.14.mask), custom_call_target="tpu_custom_call" | custom-call | tf_op jit(solution)/shard_map/pallas_call | solution.py:362
  57.5 0.0 copy-done
  57.6 55.9 %shard_map.103 = (bf16[2,16,24,1024]{3,2,1,0:T(8,128)(2,1)S(1)}, bf16[2,24,1024]{2,1,0:T(8,128)(2,1)S(1)}) custom-call(bf16[384,256]{1,0:T(8,128)(2,1)S(1)} %bitcast.18, bf16[2,256,1024]{2,1,0:T(8,128)(2,1)S(1)} %copy-done, bf16[2,16,24,1024]{3,2,1,0:T(8,128)(2,1)S(1)} %shard_map.101.resid, f32[2,1,1024]{2,1,0:T(1,128)S(1)} %broadcast_in_dim.13.bias), custom_call_target="tpu_custom_call" | custom-call | tf_op jit(solution)/shard_map/pallas_call | solution.py:372
  113.5 0.6 copy.23
  114.1 0.9 convert_reduce_fusion
  115.0 14.7 %shard_map.104 = (bf16[8,48,256]{2,1,0:T(8,128)(2,1)S(1)}, bf16[2,256,1024]{2,1,0:T(8,128)(2,1)S(1)}) custom-call(bf16[2,384,1024]{2,1,0:T(8,128)(2,1)S(1)} %bitcast.17, bf16[2,256,1024]{2,1,0:T(8,128)(2,1)S(1)} %copy-done, bf16[8,48,256]{2,1,0:T(8,128)(2,1)S(1)} %shard_map.102.act), custom_call_target="tpu_custom_call" | custom-call | tf_op jit(solution)/shard_map/pallas_call | solution.py:392
  129.8 1.7 %convolution_convert_fusion = bf16[2,1024,256]{2,1,0:T(8,128)(2,1)} fusion(bf16[2,384,1024]{2,1,0:T(8,128)(2,1)S(1)} %bitcast.16, bf16[384,256,1]{1,0,2:T(8,128)(2,1)S(1)} %bitcast.19), kind=kOutput, calls=%fused_computation.2 | convolution fusion | flops 403177472 | bytes 2818048 | tf_op jit(solution)/shard_map/ltd,tf->ldf/dot_general | solution.py:402
  131.5 0.6 convert_reduce_fusion.1
  132.1 1.0 copy.29
  (8 shorter events, 0.1 us)
Async XLA Ops:
  3.4 35.9 %copy-start.1 = (bf16[2,1024,256]{2,1,0:T(8,128)(2,1)S(1)}, bf16[2,1024,256]{2,1,0:T(8,128)(2,1)}, u32[]{:S(2)}) copy-start(bf16[2,1024,256]{2,1,0:T(8,128)(2,1)} %w.1) | copy-start | bytes 3145732
  3.4 35.9 %copy-start.2 = (f32[256]{0:T(256)S(1)}, f32[256]{0:T(256)}, u32[]{:S(2)}) copy-start(f32[256]{0:T(256)} %param.8) | copy-start | bytes 3076
  39.3 18.2 %copy-start = (bf16[2,256,1024]{2,1,0:T(8,128)(2,1)S(1)}, bf16[2,256,1024]{2,1,0:T(8,128)(2,1)}, u32[]{:S(2)}) copy-start(bf16[2,256,1024]{2,1,0:T(8,128)(2,1)} %dec.3) | copy-start | bytes 3145732
